TPU v7x, 256 devices: a whole 4x4x8 slice. The times are simulated.
256 devices in a mesh: dp: 64 (over z, x, core), mp: 4 (over y).
Axes of the slice: x: 4, y: 4, z: 8, core: 2. Of those that a mesh axis runs over, the one named last changes fastest.
Arguments:
- tokens: bfloat16 [32768, 8192], P('dp', 'mp'), may hold values from -6 to 6
- base_weight: bfloat16 [8192, 1024], P('mp'), may hold values from -0.0625 to 0.0625
- adapter_down: bfloat16 [256, 32, 8192], P('dp', None, 'mp'), may hold values from -0.0625 to 0.0625
- adapter_up: bfloat16 [256, 32, 1024], P('dp', None, 'mp'), may hold values from -1 to 1
- block_adapter: int32 [1024], P('dp'), may hold values from 0 to 255, as said below
- cotangent: bfloat16 [32768, 1024], P('dp', 'mp'), may hold values from -6 to 6
Outputs:
- output: bfloat16 [32768, 1024], P('dp', 'mp')
- input_grad: bfloat16 [32768, 8192], P('dp', 'mp')
- down_grad: float32 [256, 32, 8192], P('dp', None, 'mp')
- up_grad: float32 [256, 32, 1024], P('dp', None, 'mp')
Inputs may be any that keep to these rules, and one draw needn't show every extreme that they name: `block_adapter`: adapter a is owned by index a // 4 of dp; the 16 blocks of one index of dp name adapters of 16 different owners.
All inputs are finite; a program needn't handle non-finite values.
Results may differ from a plain program's by a relative error of at most 0.0045.
Values may be sent and summed in bfloat16 or wider, within the bound.
No kernel may reach another device: no remote copies, remote signals or barrier semaphores. Data moves between devices by JAX's collectives and lax.ppermute only.
A program may use at most 128 MiB of HBM per device.

v0:
```python
import jax
import jax.numpy as jnp
from jax import lax
from jax.sharding import PartitionSpec as P

adapter_scale = 2.0


def shards(tokens, base_weight, adapter_down, adapter_up, block_adapter, cotangent):
    blocks = block_adapter.shape[0]
    owned = adapter_down.shape[0]
    width_local = tokens.shape[1]
    local_columns = cotangent.shape[1]
    groups = lax.axis_size("dp")
    myself = lax.axis_index("dp")
    all_ids = lax.all_gather(block_adapter, "dp", axis=0, tiled=True)
    id_table = all_ids.reshape(groups, blocks)
    is_mine = id_table // owned == myself
    local_ids = id_table - myself * owned
    slots = jnp.arange(owned, dtype=jnp.int32)
    picked = jnp.any(is_mine[:, :, None] & (local_ids[:, :, None] == slots[None, None, :]), axis=1)
    pick_bf = picked.astype(jnp.bfloat16)
    pick_f32 = picked.astype(jnp.float32)
    send_down = jnp.einsum(
        "ga,ard->grd", pick_bf, adapter_down, preferred_element_type=jnp.float32
    ).astype(jnp.bfloat16)
    send_up = jnp.einsum(
        "ga,ark->grk", pick_bf, adapter_up, preferred_element_type=jnp.float32
    ).astype(jnp.bfloat16)
    recv_down = lax.all_to_all(send_down, "dp", split_axis=0, concat_axis=0, tiled=True)
    recv_up = lax.all_to_all(send_up, "dp", split_axis=0, concat_axis=0, tiled=True)
    my_owner = block_adapter // owned
    down_blk = jnp.take(recv_down, my_owner, axis=0)
    up_blk = jnp.take(recv_up, my_owner, axis=0)
    token_blk = tokens.reshape(blocks, -1, width_local)
    block_len = token_blk.shape[1]
    rank_part = jnp.einsum("btd,brd->btr", token_blk, down_blk, preferred_element_type=jnp.float32)
    rank_vals = lax.psum(rank_part, "mp").astype(jnp.bfloat16)
    base_part = jnp.dot(tokens, base_weight, preferred_element_type=jnp.float32)
    frozen_columns = lax.psum_scatter(base_part, "mp", scatter_dimension=1, tiled=True)
    adapted_output = jnp.einsum(
        "btr,brk->btk", rank_vals, up_blk, preferred_element_type=jnp.float32
    )
    output = (frozen_columns + adapter_scale * adapted_output.reshape(-1, local_columns)).astype(
        jnp.bfloat16
    )
    cot_full = lax.all_gather(cotangent, "mp", axis=1, tiled=True)
    cot_blk = cotangent.reshape(blocks, -1, local_columns)
    local_term = jnp.einsum("btk,brk->btr", cot_blk, up_blk, preferred_element_type=jnp.float32)
    rank_totals = lax.psum(local_term, "mp")
    rank_gradient = (adapter_scale * rank_totals).astype(jnp.bfloat16)
    through_base = jnp.dot(cot_full, base_weight.T, preferred_element_type=jnp.float32)
    through_down = jnp.einsum(
        "btr,brd->btd", rank_gradient, down_blk, preferred_element_type=jnp.float32
    )
    input_grad = (through_base + through_down.reshape(-1, width_local)).astype(jnp.bfloat16)
    down_terms = (
        jnp.einsum("btr,btd->brd", rank_gradient, token_blk, preferred_element_type=jnp.float32)
        / block_len
    )
    up_terms = (
        adapter_scale
        * jnp.einsum("btr,btk->brk", rank_vals, cot_blk, preferred_element_type=jnp.float32)
        / block_len
    )
    route = (my_owner[:, None] == jnp.arange(groups, dtype=jnp.int32)[None, :]).astype(jnp.float32)
    out_down = jnp.einsum("bg,brd->grd", route, down_terms, precision=lax.Precision.HIGHEST)
    out_up = jnp.einsum("bg,brk->grk", route, up_terms, precision=lax.Precision.HIGHEST)
    got_down, got_up = (
        lax.all_to_all(out_down, "dp", split_axis=0, concat_axis=0, tiled=True),
        lax.all_to_all(out_up, "dp", split_axis=0, concat_axis=0, tiled=True),
    )
    down_grad = jnp.einsum("ga,grd->ard", pick_f32, got_down, precision=lax.Precision.HIGHEST)
    up_grad = jnp.einsum("ga,grk->ark", pick_f32, got_up, precision=lax.Precision.HIGHEST)
    return (output, input_grad, down_grad, up_grad)


def solution(mesh):
    return jax.shard_map(
        shards,
        mesh=mesh,
        in_specs=(
            P("dp", "mp"),
            P("mp", None),
            P("dp", None, "mp"),
            P("dp", None, "mp"),
            P("dp"),
            P("dp", "mp"),
        ),
        out_specs=(P("dp", "mp"), P("dp", "mp"), P("dp", None, "mp"), P("dp", None, "mp")),
        check_vma=False,
    )
```

profile of v0, /device:TPU:37, one launch (start us, length us, event | category | flops | bytes accessed | tf_op | source)
XLA Modules:
  0.0 784.4 jit_solution(11181563550180228233)
XLA Ops:
  10.1 16.5 %all-reduce = s32[1024]{0:T(1024)S(1)} all-reduce(s32[1024]{0:T(1024)S(1)} %dynamic-update-slice), channel_id=1, replica_groups=mesh['dp'=64,'mp'=4] {'dp'}, use_global_device_ids=true, to_apply=%add | all-reduce | flops 1024 | bytes 8192
  26.9 6.7 convolution_convert_fusion
  33.6 11.2 %copy.64 = bf16[64,32,2048]{2,1,0:T(8,128)(2,1)} copy(bf16[64,32,2048]{2,0,1:T(8,128)(2,1)} %convolution_convert_fusion) | data formatting | bytes 16777216 | tf_op jit(solution)/shard_map/convert_element_type | solution.py:26
  44.9 12.8 %all-to-all-start = ((bf16[64,32,2048]{2,1,0:T(8,128)(2,1)}), bf16[64,32,2048]{2,1,0:T(8,128)(2,1)}, u32[]{:S(2)}, u32[]{:S(2)}) async-start(bf16[64,32,2048]{2,1,0:T(8,128)(2,1)} %copy.64), calls=%async_computation.1 | async-start | bytes 16777216 | tf_op jit(solution)/shard_map/all_to_all | solution.py:30
  59.8 184.0 %all-to-all-done = bf16[64,32,2048]{2,1,0:T(8,128)(2,1)} async-done(((bf16[64,32,2048]{2,1,0:T(8,128)(2,1)}), bf16[64,32,2048]{2,1,0:T(8,128)(2,1)}, u32[]{:S(2)}, u32[]{:S(2)}) %all-to-all-start) | async-done | bytes 8388640 | tf_op jit(solution)/shard_map/all_to_all | solution.py:30
  243.8 7.0 all-to-all-start.1
  250.8 5.4 gather_fusion
  256.2 2.4 convolution_bitcast_fusion.1
  258.6 17.6 %psum.14 = bf16[16,32,32]{1,2,0:T(8,128)(2,1)S(1)} all-reduce(f32[16,32,32]{1,2,0:T(8,128)S(1)} %convolution_bitcast_fusion.1), channel_id=1, replica_groups=mesh['dp'=64,'mp'=4] {'mp'}, use_global_device_ids=true, to_apply=%region_2.3 | all-reduce | flops 16384 | bytes 98304 | tf_op jit(solution)/shard_map/psum | solution.py:38
  277.5 2.5 copy.73
  280.0 13.7 %all-to-all-start.3 = ((f32[64,32,256]{2,1,0:T(8,128)}), f32[64,32,256]{2,1,0:T(8,128)}, u32[]{:S(2)}, u32[]{:S(2)}) async-start(f32[64,32,256]{2,1,0:T(8,128)} %copy.73), calls=%async_computation.4 | async-start | bytes 4194304 | tf_op jit(solution)/shard_map/all_to_all | solution.py:71
  296.6 45.8 %all-reduce.3.cloned.1.call-done = f32[16,32,32]{1,2,0:T(8,128)} async-done(((f32[16,32,32]{1,2,0:T(8,128)}), f32[16,32,32]{1,2,0:T(8,128)}) %all-reduce.3.cloned.1.call-update) | async-done | bytes 65552 | tf_op jit(solution)/shard_map/psum | solution.py:50
  344.1 8.3 %fusion.3 = f32[64,32,2048]{2,0,1:T(8,128)S(1)} fusion(f32[16,32,2048]{2,1,0:T(8,128)S(1)} %convolution_multiply_fusion, s32[16]{0:T(128)S(1)} %get-tuple-element.25), kind=kOutput, calls=%fused_computation.7 | convolution fusion | flops 805307392 | bytes 20971584 | tf_op jit(solution)/shard_map/bg,brd->grd/dot_general | solution.py:67
  352.3 19.2 %copy.70 = f32[64,32,2048]{2,1,0:T(8,128)} copy(f32[64,32,2048]{2,0,1:T(8,128)S(1)} %fusion.3) | data formatting | bytes 33554432 | tf_op jit(solution)/shard_map/bg,brd->grd/dot_general | solution.py:67
  371.6 12.2 %all-to-all-start.2 = ((f32[64,32,2048]{2,1,0:T(8,128)}), f32[64,32,2048]{2,1,0:T(8,128)}, u32[]{:S(2)}, u32[]{:S(2)}) async-start(f32[64,32,2048]{2,1,0:T(8,128)} %copy.70), calls=%async_computation.3 | async-start | bytes 33554432 | tf_op jit(solution)/shard_map/all_to_all | solution.py:70
  383.9 5.8 fusion.35
  390.8 31.4 %reduce-scatter.2.cloned.1.call-done = f32[512,256]{1,0:T(8,128)} async-done(((f32[512,1024]{1,0:T(8,128)}), f32[512,256]{1,0:T(8,128)}) %reduce-scatter.2.cloned.1.call-update) | async-done | bytes 524304 | tf_op jit(solution)/shard_map/reduce_scatter | solution.py:40
  422.2 1.8 fusion.8
  424.0 4.4 fusion.7
  428.4 22.1 %all-gather.2.cloned.1.call-done = bf16[512,1024]{1,0:T(8,128)(2,1)} async-done(((bf16[512,256]{1,0:T(8,128)(2,1)}), bf16[512,1024]{1,0:T(8,128)(2,1)}) %all-gather.2.cloned.1.call-update) | async-done | bytes 1048592 | tf_op jit(solution)/shard_map/all_gather | solution.py:47
  450.5 7.5 fusion.2
  457.9 3.4 fusion.5
  462.0 293.7 %all-to-all-done.2 = f32[64,32,2048]{2,1,0:T(8,128)} async-done(((f32[64,32,2048]{2,1,0:T(8,128)}), f32[64,32,2048]{2,1,0:T(8,128)}, u32[]{:S(2)}, u32[]{:S(2)}) %all-to-all-start.2) | async-done | bytes 16777248 | tf_op jit(solution)/shard_map/all_to_all | solution.py:70
  755.7 20.1 %fusion = f32[4,32,2048]{2,0,1:T(4,128)S(1)} fusion(f32[64,32,2048]{2,1,0:T(8,128)} %all-to-all-done.2, pred[64,4]{0,1:T(4,128)(4,1)S(1)} %fusion.16), kind=kOutput, calls=%fused_computation.2 | convolution fusion | flops 201326592 | bytes 17826048 | tf_op jit(solution)/shard_map/ga,grd->ard/dot_general | solution.py:73
  (40 shorter events, 13.8 us)
Async XLA Ops:
  7.2 249.0 %copy-start = (bf16[512,2048]{1,0:T(8,128)(2,1)S(1)}, bf16[512,2048]{1,0:T(8,128)(2,1)}, u32[]{:S(2)}) copy-start(bf16[512,2048]{1,0:T(8,128)(2,1)} %param.6) | copy-start | bytes 6291460
  44.9 12.9 %copy-start.3 = (bf16[4,32,256]{2,1,0:T(8,128)(2,1)S(1)}, bf16[4,32,256]{2,1,0:T(8,128)(2,1)}, u32[]{:S(2)}) copy-start(bf16[4,32,256]{2,1,0:T(8,128)(2,1)} %param.9) | copy-start | bytes 196612
  44.9 198.9 %all-to-all-start = ((bf16[64,32,2048]{2,1,0:T(8,128)(2,1)}), bf16[64,32,2048]{2,1,0:T(8,128)(2,1)}, u32[]{:S(2)}, u32[]{:S(2)}) async-start(bf16[64,32,2048]{2,1,0:T(8,128)(2,1)} %copy.64), calls=%async_computation.1 | async-start | bytes 16777216 | tf_op jit(solution)/shard_map/all_to_all | solution.py:30
  58.2 192.5 %copy-start.4 = (s32[16]{0:T(128)S(1)}, s32[16]{0:T(128)}, u32[]{:S(2)}) copy-start(s32[16]{0:T(128)} %param.10) | copy-start | bytes 196
  243.8 36.3 %all-to-all-start.1 = ((bf16[64,32,256]{2,1,0:T(8,128)(2,1)}), bf16[64,32,256]{2,1,0:T(8,128)(2,1)}, u32[]{:S(2)}, u32[]{:S(2)}) async-start(bf16[64,32,256]{2,1,0:T(8,128)(2,1)} %copy.66), calls=%async_computation.2 | async-start | bytes 2097152 | tf_op jit(solution)/shard_map/all_to_all | solution.py:31
  256.2 19.9 %copy-start.1 = (bf16[512,256]{1,0:T(8,128)(2,1)S(1)}, bf16[512,256]{1,0:T(8,128)(2,1)}, u32[]{:S(2)}) copy-start(bf16[512,256]{1,0:T(8,128)(2,1)} %param.11) | copy-start | bytes 786436
  280.0 91.5 %all-to-all-start.3 = ((f32[64,32,256]{2,1,0:T(8,128)}), f32[64,32,256]{2,1,0:T(8,128)}, u32[]{:S(2)}, u32[]{:S(2)}) async-start(f32[64,32,256]{2,1,0:T(8,128)} %copy.73), calls=%async_computation.4 | async-start | bytes 4194304 | tf_op jit(solution)/shard_map/all_to_all | solution.py:71
  293.7 48.7 %all-reduce.3.cloned.1.call-start = ((), (), s32[]{:S(2)}) async-start(), calls=%async_computation.7 | async-start | bytes 524288 | tf_op jit(solution)/shard_map/psum | solution.py:50
  371.6 384.1 %all-to-all-start.2 = ((f32[64,32,2048]{2,1,0:T(8,128)}), f32[64,32,2048]{2,1,0:T(8,128)}, u32[]{:S(2)}, u32[]{:S(2)}) async-start(f32[64,32,2048]{2,1,0:T(8,128)} %copy.70), calls=%async_computation.3 | async-start | bytes 33554432 | tf_op jit(solution)/shard_map/all_to_all | solution.py:70
  383.8 38.3 %reduce-scatter.2.cloned.1.call-start = ((), (), s32[]{:S(2)}) async-start(), calls=%async_computation.5 | async-start | bytes 2621440 | tf_op jit(solution)/shard_map/reduce_scatter | solution.py:40
  389.7 34.2 %copy-start.2 = (f32[16,32,32]{1,2,0:T(8,128)S(1)}, f32[16,32,32]{1,2,0:T(8,128)}, u32[]{:S(2)}) copy-start(f32[16,32,32]{1,2,0:T(8,128)} %all-reduce.3.cloned.1.call-done) | copy-start | bytes 196612
  389.7 60.7 %all-gather.2.cloned.1.call-start = ((), (), s32[]{:S(2)}) async-start(), calls=%async_computation.6 | async-start | bytes 1310720 | tf_op jit(solution)/shard_map/all_gather | solution.py:47
Sparse Core Ops, SparseCore 0:
  297.4 44.9 all-reduce.2
  389.9 32.2 reduce-scatter.1
  424.0 26.4 all-gather.1
where the time goes:
time: 793 us; the launch traced here: 784 us
  waiting for transfers between devices  578 us (73%)
  matrix products  63.4 us (8%)
  local copies, waits for them, and re-layouts  46.5 us (6%)
  starting transfers between devices  45.8 us (6%)
  blocking collectives  34.1 us (4%)
  between operations  15 us (2%)
    all_to_all x1, waiting for transfers between devices, shards(): lax.all_to_all(out_down, 'dp', split_axis=0, concat_axis=0, tiled=True)  294 us
    all_to_all x1, waiting for transfers between devices, shards(): lax.all_to_all(send_down, 'dp', split_axis=0, concat_axis=0, tiled=True)  184 us
    psum x1, waiting for transfers between devices, shards(): rank_totals = lax.psum(local_term, 'mp')  45.8 us
    reduce_scatter x1, waiting for transfers between devices, shards(): lax.psum_scatter(base_part, 'mp', scatter_dimension=1, tiled=True)  31.4 us
    all_gather x1, waiting for transfers between devices, shards(): cot_full = lax.all_gather(cotangent, 'mp', axis=1, tiled=True)  22.1 us
    dot_general x1, matrix products, shards(): jnp.einsum('ga,grd->ard', pick_f32, got_down, precision=lax.Precision.HIG...  20.1 us
    dot_general x1, local copies, waits for them, and re-layouts, shards(): jnp.einsum('bg,brd->grd', route, down_terms, precision=lax.Precision.HIGH...  19.2 us
    psum x1, blocking collectives, shards(): rank_vals = lax.psum(rank_part, 'mp').astype(jnp.bfloat16)  17.6 us
  transfers between devices with their start and end apart: 7, of which 5 were waited for; matrix products, arithmetic and copies ran while one was open for 9% of the time, Pallas kernels for 0%

commit v1 on v0

v1 whole, which is shorter than its diff:
```python
import jax
import jax.numpy as jnp
from jax import lax
from jax.sharding import Mesh, PartitionSpec as P

adapter_scale = 2.0
PLANE = 8


def shards(tokens, base_weight, adapter_down, adapter_up, block_adapter, cotangent):
    f32, bf = jnp.float32, jnp.bfloat16
    blocks = block_adapter.shape[0]
    owned = adapter_down.shape[0]
    width_local = tokens.shape[1]
    local_columns = cotangent.shape[1]
    dp = ("z", "g")
    planes = lax.axis_size("z")
    plane = lax.axis_size("g")
    adapters = planes * plane * owned
    narrow = width_local // plane
    block_len = tokens.shape[0] // blocks

    ids = block_adapter
    ids_plane = lax.all_gather(ids, "g", axis=0, tiled=True)

    up_all = lax.all_gather(adapter_up, dp, axis=0, tiled=True)
    up_blk = jnp.take(up_all, ids, axis=0)
    cot_blk = cotangent.reshape(blocks, block_len, local_columns)
    local_term = jnp.einsum("btk,brk->btr", cot_blk, up_blk, preferred_element_type=f32)
    rank_gradient = (adapter_scale * lax.psum(local_term, "mp")).astype(bf)
    rg_plane = lax.all_gather(rank_gradient, "g", axis=0, tiled=True)

    tok_n = lax.all_to_all(tokens, "g", split_axis=1, concat_axis=0, tiled=True)
    tok_nb = tok_n.reshape(plane * blocks, block_len, narrow)
    down_n = lax.all_to_all(adapter_down, "g", split_axis=2, concat_axis=0, tiled=True)
    table = lax.all_gather(down_n, "z", axis=0, tiled=True)
    down_nb = jnp.take(table, ids_plane, axis=0)

    down_terms = jnp.einsum("btr,btd->brd", rg_plane, tok_nb, preferred_element_type=f32) / block_len
    route = (jnp.arange(adapters, dtype=jnp.int32)[:, None] == ids_plane[None, :]).astype(f32)
    grad_table = jnp.einsum("ab,brd->ard", route, down_terms, precision=lax.Precision.HIGHEST)
    grad_n = lax.psum_scatter(grad_table.astype(bf), "z", scatter_dimension=0, tiled=True)
    down_grad = lax.all_to_all(grad_n, "g", split_axis=0, concat_axis=2, tiled=True).astype(f32)

    through_n = jnp.einsum("btr,brd->btd", rg_plane, down_nb, preferred_element_type=f32)
    through = lax.all_to_all(
        through_n.reshape(-1, narrow).astype(bf), "g", split_axis=0, concat_axis=1, tiled=True
    )

    rank_part = jnp.einsum("btd,brd->btr", tok_nb, down_nb, preferred_element_type=f32)
    rank_parts = lax.all_to_all(
        rank_part.reshape(plane, blocks, block_len, -1), "g", split_axis=0, concat_axis=0, tiled=True
    )
    rank_vals = lax.psum(jnp.sum(rank_parts, axis=0), "mp").astype(bf)

    base_part = jnp.dot(tokens, base_weight, preferred_element_type=f32)
    frozen_columns = lax.psum_scatter(base_part, "mp", scatter_dimension=1, tiled=True)
    adapted_output = jnp.einsum("btr,brk->btk", rank_vals, up_blk, preferred_element_type=f32)
    output = (frozen_columns + adapter_scale * adapted_output.reshape(-1, local_columns)).astype(bf)

    cot_full = lax.all_gather(cotangent, "mp", axis=1, tiled=True)
    through_base = jnp.dot(cot_full, base_weight.T, preferred_element_type=f32)
    input_grad = (through_base + through.astype(f32)).astype(bf)

    up_terms = (
        adapter_scale
        * jnp.einsum("btr,btk->brk", rank_vals, cot_blk, preferred_element_type=f32)
        / block_len
    )
    route_up = (jnp.arange(adapters, dtype=jnp.int32)[:, None] == ids[None, :]).astype(f32)
    up_table = jnp.einsum("ab,brk->ark", route_up, up_terms, precision=lax.Precision.HIGHEST)
    up_grad = lax.psum_scatter(up_table.astype(bf), dp, scatter_dimension=0, tiled=True).astype(f32)
    return (output, input_grad, down_grad, up_grad)


def solution(mesh):
    fine = Mesh(mesh.devices.reshape(-1, PLANE, mesh.devices.shape[1]), ("z", "g", "mp"))
    dp = ("z", "g")
    return jax.shard_map(
        shards,
        mesh=fine,
        in_specs=(
            P(dp, "mp"),
            P("mp", None),
            P(dp, None, "mp"),
            P(dp, None, "mp"),
            P(dp),
            P(dp, "mp"),
        ),
        out_specs=(P(dp, "mp"), P(dp, "mp"), P(dp, None, "mp"), P(dp, None, "mp")),
        check_vma=False,
    )
```

time: 793 us -> 393 us (0.50)
  the two profiles are of different devices: /device:TPU:37 before, /device:TPU:8 now
where the time goes in v1:
time: 393 us; the launch traced here: 392 us
  waiting for transfers between devices  209 us (53%)
  blocking collectives  72 us (18%)
  local copies, waits for them, and re-layouts  37.2 us (9%)
  matrix products  33.9 us (9%)
  between operations  16.1 us (4%)
  starting transfers between devices  15.4 us (4%)
  other arithmetic  8.59 us (2%)
    reduce_scatter x1, waiting for transfers between devices, shards(): lax.psum_scatter(up_table.astype(bf), dp, scatter_dimension=0, tiled=True)  107 us
    all_gather x1, waiting for transfers between devices, shards(): up_all = lax.all_gather(adapter_up, dp, axis=0, tiled=True)  74.8 us
    unnamed x1, blocking collectives  28.4 us
    all_to_all x1, waiting for transfers between devices, shards(): lax.all_to_all(through_n.reshape(-1, narrow).astype(bf), 'g', split_axis=...  25 us
    psum x1, blocking collectives, shards(): rank_vals = lax.psum(jnp.sum(rank_parts, axis=0), 'mp').astype(bf)  17 us
    unnamed x18, local copies, waits for them, and re-layouts  14.7 us
    all_gather x1, blocking collectives, shards(): rg_plane = lax.all_gather(rank_gradient, 'g', axis=0, tiled=True)  13.8 us
    all_to_all x1, blocking collectives, shards(): lax.all_to_all(rank_part.reshape(plane, blocks, block_len, -1), 'g', spli...  12.9 us
  transfers between devices with their start and end apart: 11, of which 3 were waited for; matrix products, arithmetic and copies ran while one was open for 19% of the time, Pallas kernels for 0%

profile of v1, /device:TPU:8, one launch (start us, length us, event | category | flops | bytes accessed | tf_op | source)
XLA Modules:
  0.0 391.9 jit_solution(15901385996979056095)
XLA Ops:
  8.7 2.8 copy.29
  11.6 2.7 reshape.79
  14.2 4.3 %all-to-all-start = ((bf16[8,2,16384]{2,1,0:T(2,128)(2,1)}), bf16[8,2,16384]{2,1,0:T(2,128)(2,1)S(1)}, u32[]{:S(2)}, u32[]{:S(2)}) async-start(bf16[8,2,16384]{2,1,0:T(2,128)(2,1)} %reshape.79), calls=%async_computation.1 | async-start | bytes 1048576 | tf_op jit(solution)/shard_map/all_to_all | solution.py:35
  18.6 74.8 %all-gather.6.cloned.1.call-done = bf16[256,32,256]{2,1,0:T(8,128)(2,1)} async-done(((bf16[4,32,256]{2,1,0:T(8,128)(2,1)}), bf16[256,32,256]{2,1,0:T(8,128)(2,1)}) %all-gather.6.cloned.1.call-update) | async-done | bytes 4194320 | tf_op jit(solution)/shard_map/all_gather | solution.py:26
  93.5 2.7 gather_fusion.1
  100.5 6.5 %fusion.20 = f32[512,1024]{1,0:T(8,128)} fusion(bf16[512,2048]{1,0:T(8,128)(2,1)} %param.6, bf16[2048,1024]{1,0:T(8,128)(2,1)} %param.7), kind=kOutput, calls=%fused_computation.41 | convolution fusion | flops 2147483648 | bytes 8388608 | tf_op jit(solution)/shard_map/dot_general | solution.py:56
  110.0 3.7 all-to-all-start.1
  115.3 28.4 %all-reduce = s32[128]{0:T(128)S(1)} all-reduce(s32[128]{0:T(128)S(1)} %dynamic-update-slice), channel_id=1, replica_groups=mesh['z'=8,'g'=8,'mp'=4] {'g'}, use_global_device_ids=true, to_apply=%add | all-reduce | flops 128 | bytes 1024
  144.8 13.8 %all_gather.19 = bf16[128,32,32]{2,1,0:T(8,128)(2,1)S(1)} all-gather(bf16[16,32,32]{2,1,0:T(8,128)(2,1)S(1)} %copy.34), channel_id=1, replica_groups=mesh['z'=8,'g'=8,'mp'=4] {'g'}, dimensions={0}, use_global_device_ids=true | all-gather | bytes 294912 | tf_op jit(solution)/shard_map/all_gather | solution.py:31
  159.4 6.9 %fusion.2 = bf16[256,32,256]{2,0,1:T(8,128)(2,1)} fusion(f32[128,32,256]{2,1,0:T(8,128)S(1)} %convolution_multiply_fusion, s32[128]{0:T(128)S(1)} %all-reduce), kind=kOutput, calls=%fused_computation.7 | convolution fusion | flops 3223355392 | bytes 8389120 | tf_op jit(solution)/shard_map/ab,brd->ard/dot_general | solution.py:41
  167.0 4.3 %gather_fusion = bf16[128,32,256]{2,1,0:T(8,128)(2,1)} fusion(bf16[256,32,256]{2,1,0:T(8,128)(2,1)} %all-gather.4.cloned.1.call-done, s32[1024]{0:T(1024)S(1)} %pad_clamp_fusion.1), kind=kCustom, calls=%fused_computation | custom fusion | bytes 4194816 | tf_op jit(solution)/shard_map/jit(_take)/gather | solution.py:37
  171.2 3.7 fusion.5
  175.0 2.5 reshape.81
  177.4 12.9 %all_to_all.58 = f32[8,1,16384]{2,1,0:T(1,128)S(1)} all-to-all(f32[8,1,16384]{2,1,0:T(1,128)S(1)} %reshape.81), channel_id=1, replica_groups=mesh['z'=8,'g'=8,'mp'=4] {'g'}, dimensions={0} | all-to-all | bytes 1048576 | tf_op jit(solution)/shard_map/all_to_all | solution.py:51
  190.8 2.8 reduce
  197.4 17.0 %psum.14 = bf16[16,32,32]{2,1,0:T(8,128)(2,1)S(1)} all-reduce(f32[16,32,32]{2,1,0:T(8,128)S(1)} %copy.33), channel_id=1, replica_groups=mesh['z'=8,'g'=8,'mp'=4] {'mp'}, use_global_device_ids=true, to_apply=%region_2.3 | all-reduce | flops 16384 | bytes 98304 | tf_op jit(solution)/shard_map/psum | solution.py:54
  215.6 3.9 convolution_convert_fusion
  219.5 4.4 %copy.42 = bf16[256,32,256]{2,1,0:T(8,128)(2,1)} copy(bf16[256,32,256]{2,0,1:T(8,128)(2,1)S(1)} %convolution_convert_fusion) | data formatting | bytes 8388608 | tf_op jit(solution)/shard_map/convert_element_type | solution.py:72
  227.6 3.6 all-to-all-start.3
  233.3 25.0 %all-to-all-done.3 = bf16[8,512,256]{2,1,0:T(8,128)(2,1)S(1)} async-done(((bf16[8,512,256]{2,1,0:T(8,128)(2,1)}), bf16[8,512,256]{2,1,0:T(8,128)(2,1)S(1)}, u32[]{:S(2)}, u32[]{:S(2)}) %all-to-all-start.3) | async-done | bytes 2097184 | tf_op jit(solution)/shard_map/all_to_all | solution.py:46
  258.7 2.6 copy.48
  263.4 3.5 all-to-all-start.4
  266.9 7.6 %add_convert_fusion = bf16[512,2048]{1,0:T(8,128)(2,1)} fusion(f32[512,2048]{1,0:T(8,128)} %bitcast.64, bf16[512,1024]{1,0:T(8,128)(2,1)} %all-gather.8.cloned.1.call-done, bf16[2048,1024]{1,0:T(8,128)(2,1)} %param.7), kind=kOutput, calls=%fused_computation.5 | convolution fusion | flops 2149580800 | bytes 11534336 | tf_op jit(solution)/shard_map/dot_general | solution.py:62
  274.6 107.4 %reduce-scatter.8.cloned.1.call-done = bf16[4,32,256]{2,1,0:T(8,128)(2,1)} async-done(((bf16[256,32,256]{2,1,0:T(8,128)(2,1)}), bf16[4,32,256]{2,1,0:T(8,128)(2,1)}) %reduce-scatter.8.cloned.1.call-update) | async-done | bytes 65552 | tf_op jit(solution)/shard_map/reduce_scatter | solution.py:72
  (61 shorter events, 28.0 us)
Async XLA Ops:
  8.0 85.5 %all-gather.6.cloned.1.call-start = ((), (), s32[]{:S(2)}) async-start(), calls=%async_computation.10 | async-start | bytes 4259840 | tf_op jit(solution)/shard_map/all_gather | solution.py:26
  11.5 7.0 %copy-start.3 = (s32[16]{0:T(128)S(1)}, s32[16]{0:T(128)}, u32[]{:S(2)}) copy-start(s32[16]{0:T(128)} %param.10) | copy-start | bytes 196
  11.6 84.7 %copy-start.1 = (bf16[512,256]{1,0:T(8,128)(2,1)S(1)}, bf16[512,256]{1,0:T(8,128)(2,1)}, u32[]{:S(2)}) copy-start(bf16[512,256]{1,0:T(8,128)(2,1)} %param.11) | copy-start | bytes 786436
  14.2 83.1 %all-to-all-start = ((bf16[8,2,16384]{2,1,0:T(2,128)(2,1)}), bf16[8,2,16384]{2,1,0:T(2,128)(2,1)S(1)}, u32[]{:S(2)}, u32[]{:S(2)}) async-start(bf16[8,2,16384]{2,1,0:T(2,128)(2,1)} %reshape.79), calls=%async_computation.1 | async-start | bytes 1048576 | tf_op jit(solution)/shard_map/all_to_all | solution.py:35
  18.5 125.2 %all-reduce.3.cloned.1.call-start = ((), (), s32[]{:S(2)}) async-start(), calls=%async_computation.12 | async-start | bytes 524288 | tf_op jit(solution)/shard_map/psum | solution.py:30
  97.3 69.7 %all-gather.4.cloned.1.call-start = ((), (), s32[]{:S(2)}) async-start(), calls=%async_computation.9 | async-start | bytes 4718592 | tf_op jit(solution)/shard_map/all_gather | solution.py:36
  100.4 131.1 %reduce-scatter.4.cloned.1.call-start = ((), (), s32[]{:S(2)}) async-start(), calls=%async_computation.8 | async-start | bytes 2621440 | tf_op jit(solution)/shard_map/reduce_scatter | solution.py:57
  107.0 1.6 copy-start.2
  110.0 3.8 copy-start.4
  110.0 48.6 %all-to-all-start.1 = ((bf16[512,8,256]{2,0,1:T(8,128)(2,1)}), bf16[512,8,256]{2,0,1:T(8,128)(2,1)S(1)}, u32[]{:S(2)}, u32[]{:S(2)}) async-start(bf16[512,8,256]{2,0,1:T(8,128)(2,1)} %bitcast.62), calls=%async_computation.2 | async-start | bytes 4194304 | tf_op jit(solution)/shard_map/all_to_all | solution.py:33
  113.8 147.5 %reduce-scatter.6.cloned.1.call-start = ((), (), s32[]{:S(2)}) async-start(), calls=%async_computation.13 | async-start | bytes 4718592 | tf_op jit(solution)/shard_map/reduce_scatter | solution.py:42
  166.2 100.7 %all-gather.8.cloned.1.call-start = ((), (), s32[]{:S(2)}) async-start(), calls=%async_computation.11 | async-start | bytes 1310720 | tf_op jit(solution)/shard_map/all_gather | solution.py:61
  166.8 215.2 %reduce-scatter.8.cloned.1.call-start = ((), (), s32[]{:S(2)}) async-start(), calls=%async_computation.14 | async-start | bytes 4259840 | tf_op jit(solution)/shard_map/reduce_scatter | solution.py:72
  223.9 1.6 copy-start
  227.6 30.7 %all-to-all-start.3 = ((bf16[8,512,256]{2,1,0:T(8,128)(2,1)}), bf16[8,512,256]{2,1,0:T(8,128)(2,1)S(1)}, u32[]{:S(2)}, u32[]{:S(2)}) async-start(bf16[8,512,256]{2,1,0:T(8,128)(2,1)} %bitcast.63), calls=%async_computation.4 | async-start | bytes 4194304 | tf_op jit(solution)/shard_map/all_to_all | solution.py:46
  263.4 120.1 %all-to-all-start.4 = ((bf16[32,32,256]{2,1,0:T(8,128)(2,1)}), bf16[32,32,256]{2,1,0:T(8,128)(2,1)S(1)}, u32[]{:S(2)}, u32[]{:S(2)}) async-start(bf16[32,32,256]{2,1,0:T(8,128)(2,1)} %copy.38), calls=%async_computation.6 | async-start | bytes 1048576 | tf_op jit(solution)/shard_map/all_to_all | solution.py:43
Sparse Core Ops, SparseCore 0:
  11.6 81.8 all-gather.5
  97.4 43.0 all-reduce.2
  143.6 32.6 reduce-scatter.3
  178.7 56.3 reduce-scatter.5
  239.0 142.9 reduce-scatter.7
Sparse Core Ops, SparseCore 1:
  100.5 51.9 all-gather.3
  168.5 25.1 all-gather.7
